TPU v7x, 32 devices: a whole 2x2x4 slice. The times are simulated.
32 devices in a mesh: occi: 4 (over y, x), occj: 8 (over z, core).
Axes of the slice: x: 2, y: 2, z: 4, core: 2. Of those that a mesh axis runs over, the one named last changes fastest.
Arguments:
- amplitudes: bfloat16 [8, 8, 512, 512], P('occi', 'occj'), may hold values from -6 to 6
- exch_int: bfloat16 [8, 8, 512, 512], P('occi', 'occj'), may hold values from -6 to 6
- thc_factor: bfloat16 [512, 2048], replicated, may hold values from -0.25 to 0.25
- thc_core: bfloat16 [2048, 2048], replicated, may hold values from -1.5 to 1.5
- fock_vir: bfloat16 [512, 512], replicated, may hold values from -0.25 to 0.25
- eps_vir: float32 [512], replicated, may hold values from 0.5 to 3
- eps_occ: float32 [8], replicated, may hold values from -1.5 to -0.2
- fock_occ: float32 [8, 8], replicated, may hold values from -1.8 to 1.8
- couple_list: int32 [8, 6], replicated, may hold values from 0 to 7, as said below
- couple_count: int32 [8], replicated, may hold values from 1 to 6, as said below
Outputs:
- residual: float32 [8, 8, 512, 512], P('occi', 'occj')
- amplitudes_new: bfloat16 [8, 8, 512, 512], P('occi', 'occj')
Inputs may be any that keep to these rules, and one draw needn't show every extreme that they name: `couple_list`: row j holds 6 distinct orbitals, none of them j. `couple_count`: some row uses all 6 entries.
All inputs are finite; a program needn't handle non-finite values.
Results may differ from a plain program's by a relative error of at most 0.0045.
Values may be sent and summed in bfloat16 or wider, within the bound.
A program may use at most 128 MiB of HBM per device.

v0:
```python
import jax
import jax.numpy as jnp
from jax import lax
from jax.sharding import PartitionSpec as P


def coupling(fock_occ, couple_list, couple_count):
    n_occ = fock_occ.shape[0]
    slots = jnp.arange(couple_list.shape[1], dtype=jnp.int32)
    active = slots[None, :] < couple_count[:, None]
    target = jnp.arange(n_occ, dtype=jnp.int32)
    hits = (couple_list[:, :, None] == target[None, None, :]) & active[:, :, None]
    return fock_occ * jnp.sum(hits.astype(fock_occ.dtype), axis=1)


def pair_terms(amp_pair, integral, thc_factor, thc_core, fock_vir):
    first = jnp.dot(amp_pair, thc_factor, preferred_element_type=jnp.float32).astype(jnp.bfloat16)
    middle = lax.dot_general(
        thc_factor, first, (((0,), (0,)), ((), ())), preferred_element_type=jnp.float32
    )
    scaled = (thc_core * middle).astype(jnp.bfloat16)
    second = jnp.dot(thc_factor, scaled, preferred_element_type=jnp.float32).astype(jnp.bfloat16)
    ladder = lax.dot_general(
        second, thc_factor, (((1,), (1,)), ((), ())), preferred_element_type=jnp.float32
    )
    virtual = jnp.dot(fock_vir, amp_pair, preferred_element_type=jnp.float32)
    return integral.astype(jnp.float32) + ladder + virtual


def shards(
    amplitudes,
    exch_int,
    thc_factor,
    thc_core,
    fock_vir,
    eps_vir,
    eps_occ,
    fock_occ,
    couple_list,
    couple_count,
):
    rows_i = amplitudes.shape[0]
    virt = amplitudes.shape[2]
    n_first = lax.axis_size("occi")
    n_second = lax.axis_size("occj")
    width = virt // (n_first * n_second)
    first_index = lax.axis_index("occi")
    second_index = lax.axis_index("occj")
    weights = coupling(fock_occ, couple_list, couple_count)
    pairs_here = amplitudes.reshape(rows_i, virt, virt)
    integrals = exch_int.reshape(rows_i, virt, virt)
    row_weights = lax.dynamic_slice_in_dim(weights, second_index, 1, 0)[0]
    empty = jnp.zeros((rows_i, virt, virt), jnp.float32)
    occupied = empty - jnp.einsum(
        "k,skab->sab",
        row_weights,
        lax.all_gather(amplitudes, "occj", axis=1, tiled=True).astype(jnp.float32),
        precision=lax.Precision.HIGHEST,
    )
    half = lax.map(
        lambda pair_in: pair_terms(pair_in[0], pair_in[1], thc_factor, thc_core, fock_vir),
        (pairs_here, integrals),
    )
    half = half + occupied
    spread = lax.all_to_all(
        half.astype(jnp.bfloat16), ("occi", "occj"), split_axis=1, concat_axis=0, tiled=True
    ).astype(half.dtype)
    mirror_part = spread.reshape(n_first, n_second, rows_i, width, virt)
    outgoing = mirror_part.reshape(n_first, n_first, rows_i, rows_i, width, virt)
    outgoing = outgoing.transpose(1, 0, 3, 2, 5, 4).reshape(
        n_first * n_second * rows_i, virt, width
    )
    mirrored = lax.all_to_all(
        outgoing.astype(jnp.bfloat16), ("occi", "occj"), split_axis=0, concat_axis=2, tiled=True
    ).astype(outgoing.dtype)
    residual = half + mirrored
    occ_rows = lax.dynamic_slice_in_dim(eps_occ, first_index * rows_i, rows_i, 0)
    occ_column = lax.dynamic_slice_in_dim(eps_occ, second_index, 1, 0)
    denominator = (
        eps_vir[None, :, None] + eps_vir[None, None, :] - occ_rows[:, None, None] - occ_column[0]
    )
    updated = (pairs_here.astype(jnp.float32) - residual / denominator).astype(jnp.bfloat16)
    return (residual.reshape(rows_i, 1, virt, virt), updated.reshape(rows_i, 1, virt, virt))


def solution(mesh):
    placed = (
        P("occi", "occj", None, None),
        P("occi", "occj", None, None),
        P(),
        P(),
        P(),
        P(),
        P(),
        P(),
        P(),
        P(),
    )
    return jax.shard_map(
        shards,
        mesh=mesh,
        in_specs=placed,
        out_specs=(P("occi", "occj", None, None), P("occi", "occj", None, None)),
        check_vma=False,
    )
```

profile of v0, /device:TPU:3, one launch (start us, length us, event | category | flops | bytes accessed | tf_op | source)
XLA Modules:
  0.0 198.8 jit_solution(14844848120025527692)
XLA Ops:
  7.2 0.7 all-gather.2.cloned.1.call-update
  7.9 0.8 copy.47
  8.7 12.4 %copy.45 = bf16[2048,2048]{0,1:T(8,128)(2,1)} copy(bf16[2048,2048]{1,0:T(8,128)(2,1)} %param.15) | data formatting | bytes 16777216 | tf_op jit(solution)/shard_map/while | solution.py:60
  21.2 48.8 %while.11 = (s32[]{:T(128)}, f32[2,512,512]{1,2,0:T(8,128)}, bf16[2,512,512]{2,1,0:T(8,128)(2,1)}, bf16[2048,2048]{0,1:T(8,128)(2,1)}, bf16[2,512,512]{2,1,0:T(8...) while((s32[]{:T(128)}, f32[2,512,512]{1,2,0:T(8,128)}, ...), condition=%wide.region_1.2_spmd.clone, body=%wide.region_0.0_spmd.sunk.clone | while | flops 11021320192 | bytes 42993232 | solution.py:60
  21.3 11.1 %fusion.55 = bf16[2048,2048]{0,1:T(8,128)(2,1)} fusion(bf16[2048,2048]{0,1:T(8,128)(2,1)} %get-tuple-element.168, bf16[512,2048]{1,0:T(8,128)(2,1)} %get-tuple-element.170, bf16[2,512,512]{2,1,0:T(8,128)(2,1)S(1)} %get-tuple-element.169, s32[]{:T(128)} %get-tuple-element.158), kind=kOutput, calls=%fused_computation.1.clone.1.clone | convolution fusion | flops 5382340608 | bytes 21496320 | tf_op jit(solution)/shard_map/while/body/eval_jaxpr/dot_general | solution.py:18
  32.3 10.4 %convolution_add_fusion.3 = f32[512,512]{1,0:T(8,128)S(1)} fusion(bf16[512,2048]{1,0:T(8,128)(2,1)} %get-tuple-element.170, bf16[2048,2048]{0,1:T(8,128)(2,1)} %fusion.55, bf16[2,512,512]{2,1,0:T(8,128)(2,1)} %get-tuple-element.167, s32[]{:T(128)} %get-tuple-element.158), kind=kOutput, calls=%fused_computation.7.clone.1.clone | convolution fusion | flops 5370281984 | bytes 14156288 | tf_op jit(solution)/shard_map/while/body/eval_jaxpr/dot_general | solution.py:23
  42.7 1.5 fusion.56
  44.2 0.3 copy.69
  44.5 1.0 constant_dynamic-update-slice_fusion.3
  45.6 11.1 %fusion.55 = bf16[2048,2048]{0,1:T(8,128)(2,1)} fusion(bf16[2048,2048]{0,1:T(8,128)(2,1)} %get-tuple-element.168, bf16[512,2048]{1,0:T(8,128)(2,1)} %get-tuple-element.170, bf16[2,512,512]{2,1,0:T(8,128)(2,1)S(1)} %get-tuple-element.169, s32[]{:T(128)} %get-tuple-element.158), kind=kOutput, calls=%fused_computation.1.clone.1.clone | convolution fusion | flops 5382340608 | bytes 21496320 | tf_op jit(solution)/shard_map/while/body/eval_jaxpr/dot_general | solution.py:18
  56.7 10.5 %convolution_add_fusion.3 = f32[512,512]{1,0:T(8,128)S(1)} fusion(bf16[512,2048]{1,0:T(8,128)(2,1)} %get-tuple-element.170, bf16[2048,2048]{0,1:T(8,128)(2,1)} %fusion.55, bf16[2,512,512]{2,1,0:T(8,128)(2,1)} %get-tuple-element.167, s32[]{:T(128)} %get-tuple-element.158), kind=kOutput, calls=%fused_computation.7.clone.1.clone | convolution fusion | flops 5370281984 | bytes 14156288 | tf_op jit(solution)/shard_map/while/body/eval_jaxpr/dot_general | solution.py:23
  67.2 1.5 fusion.56
  68.7 0.3 copy.69
  69.0 1.0 constant_dynamic-update-slice_fusion.3
  70.0 23.2 %all-gather.2.cloned.1.call-done = bf16[2,8,512,512]{3,2,1,0:T(8,128)(2,1)} async-done(((bf16[2,1,512,512]{3,2,1,0:T(8,128)(2,1)}), bf16[2,8,512,512]{3,2,1,0:T(8,128)(2,1)}) %all-gather.2.cloned.1.call-update) | async-done | bytes 8388624 | tf_op jit(solution)/shard_map/all_gather | solution.py:57
  93.3 14.3 %fusion.12 = f32[1,2,512,512]{3,0,2,1:T(1,128)} fusion(bf16[2,8,512,512]{3,2,1,0:T(8,128)(2,1)} %all-gather.2.cloned.1.call-done, f32[8,8]{1,0:T(8,128)S(1)} %mul.9, s32[]{:T(128)S(6)} %select_n.7), kind=kOutput, calls=%fused_computation.15 | convolution fusion | flops 50331648 | bytes 10486276 | tf_op jit(solution)/shard_map/k,skab->sab/dot_general | solution.py:54
  107.6 4.6 %copy.59 = f32[1,2,512,512]{2,3,1,0:T(8,128)S(1)} copy(f32[1,2,512,512]{3,0,2,1:T(1,128)} %fusion.12) | data formatting | bytes 4194304 | tf_op jit(solution)/shard_map/k,skab->sab/dot_general | solution.py:54
  112.2 3.1 %fusion.16 = bf16[2,512,512]{1,2,0:T(8,128)(2,1)} fusion(f32[2,512,512]{1,2,0:T(8,128)} %get-tuple-element.39, f32[1,2,512,512]{2,3,1,0:T(8,128)S(1)} %copy.59), kind=kLoop, calls=%fused_computation.23 | loop fusion | flops 1572864 | bytes 5242880 | tf_op jit(solution)/shard_map/convert_element_type | solution.py:66
  115.3 3.7 %copy.49 = bf16[2,512,512]{2,0,1:T(2,128)(2,1)} copy(bf16[2,512,512]{1,2,0:T(8,128)(2,1)} %fusion.16) | data formatting | bytes 2097152 | tf_op jit(solution)/shard_map/convert_element_type | solution.py:66
  118.9 29.8 %all_to_all.8 = bf16[2,512,512]{2,0,1:T(2,128)(2,1)S(1)} all-to-all(bf16[2,512,512]{2,0,1:T(2,128)(2,1)} %copy.49), channel_id=1, replica_groups=mesh['occi'=4,'occj'=8] {'occi','occj'}, dimensions={1} | all-to-all | bytes 2097152 | tf_op jit(solution)/shard_map/all_to_all | solution.py:65
  148.9 1.1 copy.52
  150.0 4.3 %all-to-all-start.1 = ((bf16[64,512,16]{1,2,0:T(8,128)(2,1)}), bf16[64,512,16]{1,2,0:T(8,128)(2,1)}, u32[]{:S(2)}, u32[]{:S(2)}) async-start(bf16[64,512,16]{1,2,0:T(8,128)(2,1)} %bitcast.107), calls=%async_computation.1 | async-start | bytes 2097152 | tf_op jit(solution)/shard_map/all_to_all | solution.py:73
  154.3 1.3 copy.43
  155.6 0.6 dynamic_slice.18
  156.4 24.6 %all-to-all-done.1 = bf16[64,512,16]{1,2,0:T(8,128)(2,1)} async-done(((bf16[64,512,16]{1,2,0:T(8,128)(2,1)}), bf16[64,512,16]{1,2,0:T(8,128)(2,1)}, u32[]{:S(2)}, u32[]{:S(2)}) %all-to-all-start.1) | async-done | bytes 1048608 | tf_op jit(solution)/shard_map/all_to_all | solution.py:73
  181.0 1.5 convert_bitcast_fusion
  182.5 0.3 copy.53
  182.8 1.3 copy-done.1
  184.1 0.3 copy-done.2
  184.4 3.3 %fusion.15 = (bf16[2,1,512,512]{2,3,0,1:T(8,128)(2,1)}, f32[2,512,512]{1,2,0:T(8,128)}) fusion(f32[]{:T(128)} %bitcast.22, f32[2]{0:T(128)S(1)} %dynamic_slice.17, f32[512,512]{0,1:T(8,128)S(1)} %broadcast_add_fusion, bf16[2,1,512,512]{2,3,0,1:T(8,128)(2,1)S(1)} %copy-done.2, f32[2,512,32,16]{1,3,2,0:T(8,128)S(1)} %copy.53, f32[2,512,512]{1,2,0:T(8,128)S(1)} %copy-done.1, ...), kind=kLoop, calls=%fused_computation.22 | loop fusion | flops 4718592 | bytes 11534348 | tf_op jit(solution)/shard_map/reshape | solution.py:83
  187.7 3.0 %copy.54 = f32[2,1,512,512]{3,2,1,0:T(8,128)} copy(f32[2,1,512,512]{2,3,0,1:T(8,128)} %bitcast.106) | data formatting | bytes 4194304
  190.6 1.3 copy.55
  (22 shorter events, 0.5 us)
Async XLA Ops:
  7.2 86.1 %all-gather.2.cloned.1.call-start = ((), (), s32[]{:S(2)}) async-start(), calls=%async_computation.2 | async-start | bytes 9437184 | tf_op jit(solution)/shard_map/all_gather | solution.py:57
  8.7 12.4 %copy-start.6 = (s32[8]{0:T(128)S(1)}, s32[8]{0:T(128)}, u32[]{:S(2)}) copy-start(s32[8]{0:T(128)} %param.21) | copy-start | bytes 100
  8.7 12.5 %copy-start.5 = (f32[8,8]{1,0:T(8,128)S(1)}, f32[8,8]{1,0:T(8,128)}, u32[]{:S(2)}) copy-start(f32[8,8]{1,0:T(8,128)} %param.19) | copy-start | bytes 772
  8.7 12.6 %copy-start = (bf16[2,1,512,512]{3,2,1,0:T(8,128)(2,1)S(1)}, bf16[2,1,512,512]{3,2,1,0:T(8,128)(2,1)}, u32[]{:S(2)}) copy-start(bf16[2,1,512,512]{3,2,1,0:T(8,128)(2,1)} %param.12) | copy-start | bytes 3145732
  150.0 5.6 %copy-start.7 = (f32[8]{0:T(128)S(1)}, f32[8]{0:T(128)}, u32[]{:S(2)}) copy-start(f32[8]{0:T(128)} %param.18) | copy-start | bytes 100
  150.0 6.2 %copy-start.4 = (f32[512]{0:T(512)S(1)}, f32[512]{0:T(512)}, u32[]{:S(2)}) copy-start(f32[512]{0:T(512)} %param.17) | copy-start | bytes 6148
  150.0 31.0 %all-to-all-start.1 = ((bf16[64,512,16]{1,2,0:T(8,128)(2,1)}), bf16[64,512,16]{1,2,0:T(8,128)(2,1)}, u32[]{:S(2)}, u32[]{:S(2)}) async-start(bf16[64,512,16]{1,2,0:T(8,128)(2,1)} %bitcast.107), calls=%async_computation.1 | async-start | bytes 2097152 | tf_op jit(solution)/shard_map/all_to_all | solution.py:73
  182.5 1.6 copy-start.1
  182.5 1.8 copy-start.2
  187.7 3.0 %copy-start.3 = (bf16[2,1,512,512]{2,3,0,1:T(8,128)(2,1)S(1)}, bf16[2,1,512,512]{2,3,0,1:T(8,128)(2,1)}, u32[]{:S(2)}) copy-start(bf16[2,1,512,512]{2,3,0,1:T(8,128)(2,1)} %get-tuple-element.90) | copy-start | bytes 3145732
Sparse Core Ops, SparseCore 0:
  9.6 83.6 all-gather.1
where the time goes:
time: 202 us; the launch traced here: 199 us
  matrix products  60.3 us (30%)
  waiting for transfers between devices  48.5 us (24%)
  local copies, waits for them, and re-layouts  33.5 us (17%)
  blocking collectives  29.8 us (15%)
  between operations  14.1 us (7%)
  other arithmetic  8.14 us (4%)
  starting transfers between devices  4.29 us (2%)
    all_to_all x1, blocking collectives, shards(): lax.all_to_all(half.astype(jnp.bfloat16), ('occi', 'occj'), split_axis=1,...  29.8 us
    all_to_all x1, waiting for transfers between devices, shards(): lax.all_to_all(outgoing.astype(jnp.bfloat16), ('occi', 'occj'), split_axi...  24.6 us
    all_gather x1, waiting for transfers between devices, shards(): lax.all_gather(amplitudes, 'occj', axis=1, tiled=True).astype(jnp.float32)  23.2 us
    dot_general x2, matrix products, pair_terms(): lax.dot_general(thc_factor, first, (((0,), (0,)), ((), ())), preferred_el...  22.2 us
    dot_general x2, matrix products, pair_terms(): lax.dot_general(second, thc_factor, (((1,), (1,)), ((), ())), preferred_e...  20.9 us
    dot_general x1, matrix products, shards(): jnp.einsum('k,skab->sab', row_weights, lax.all_gather(amplitudes, 'occj',...  14.3 us
    while x1, local copies, waits for them, and re-layouts, shards(): lax.map(lambda pair_in: pair_terms(pair_in[0], pair_in[1], thc_factor, th...  12.4 us
    unnamed x20, local copies, waits for them, and re-layouts  7.98 us
  transfers between devices with their start and end apart: 2, of which 2 were waited for; matrix products, arithmetic and copies ran while one was open for 32% of the time, Pallas kernels for 0%

commit v1 on v0

--- a/solution.py
+++ b/solution.py
@@ -43,37 +43,34 @@
     virt = amplitudes.shape[2]
     n_first = lax.axis_size("occi")
     n_second = lax.axis_size("occj")
-    width = virt // (n_first * n_second)
     first_index = lax.axis_index("occi")
     second_index = lax.axis_index("occj")
     weights = coupling(fock_occ, couple_list, couple_count)
     pairs_here = amplitudes.reshape(rows_i, virt, virt)
     integrals = exch_int.reshape(rows_i, virt, virt)
     row_weights = lax.dynamic_slice_in_dim(weights, second_index, 1, 0)[0]
-    empty = jnp.zeros((rows_i, virt, virt), jnp.float32)
-    occupied = empty - jnp.einsum(
-        "k,skab->sab",
-        row_weights,
-        lax.all_gather(amplitudes, "occj", axis=1, tiled=True).astype(jnp.float32),
-        precision=lax.Precision.HIGHEST,
-    )
-    half = lax.map(
-        lambda pair_in: pair_terms(pair_in[0], pair_in[1], thc_factor, thc_core, fock_vir),
-        (pairs_here, integrals),
-    )
-    half = half + occupied
-    spread = lax.all_to_all(
-        half.astype(jnp.bfloat16), ("occi", "occj"), split_axis=1, concat_axis=0, tiled=True
-    ).astype(half.dtype)
-    mirror_part = spread.reshape(n_first, n_second, rows_i, width, virt)
-    outgoing = mirror_part.reshape(n_first, n_first, rows_i, rows_i, width, virt)
-    outgoing = outgoing.transpose(1, 0, 3, 2, 5, 4).reshape(
-        n_first * n_second * rows_i, virt, width
-    )
-    mirrored = lax.all_to_all(
-        outgoing.astype(jnp.bfloat16), ("occi", "occj"), split_axis=0, concat_axis=2, tiled=True
-    ).astype(outgoing.dtype)
-    residual = half + mirrored
+    gathered = lax.all_gather(amplitudes, "occj", axis=1, tiled=True)
+    ladders = [
+        pair_terms(pairs_here[s], integrals[s], thc_factor, thc_core, fock_vir)
+        for s in range(rows_i)
+    ]
+    half = jnp.stack(ladders)
+    for k in range(n_second):
+        half = half - row_weights[k] * gathered[:, k].astype(jnp.float32)
+    turned = half.astype(jnp.bfloat16).transpose(0, 2, 1)
+    mirrored = jnp.zeros_like(turned)
+    for t in range(rows_i):
+        hops = []
+        for a in range(n_first):
+            for j in range(n_second):
+                s = (j + t) % rows_i
+                hops.append((a * n_second + j, (j // rows_i) * n_second + a * rows_i + s))
+        sent = lax.dynamic_index_in_dim(turned, (second_index + t) % rows_i, 0, keepdims=False)
+        got = lax.ppermute(sent, ("occi", "occj"), hops)
+        mirrored = lax.dynamic_update_index_in_dim(
+            mirrored, got, (second_index + rows_i - t) % rows_i, 0
+        )
+    residual = half + mirrored.astype(jnp.float32)
     occ_rows = lax.dynamic_slice_in_dim(eps_occ, first_index * rows_i, rows_i, 0)
     occ_column = lax.dynamic_slice_in_dim(eps_occ, second_index, 1, 0)
     denominator = (
@@ -84,18 +81,7 @@
 
 
 def solution(mesh):
-    placed = (
-        P("occi", "occj", None, None),
-        P("occi", "occj", None, None),
-        P(),
-        P(),
-        P(),
-        P(),
-        P(),
-        P(),
-        P(),
-        P(),
-    )
+    placed = (P("occi", "occj", None, None),) * 2 + (P(),) * 8
     return jax.shard_map(
         shards,
         mesh=mesh,

time: 202 us -> 201 us (level); the launches traced: 199 us -> 200 us
  waiting for transfers between devices: 48.5 us -> 91.5 us
  blocking collectives: 29.8 us -> 0 us
  matrix products: 60.3 us -> 46.5 us
  other arithmetic: 8.14 us -> 21.7 us
  local copies, waits for them, and re-layouts: 33.5 us -> 21.8 us
    ppermute x0 -> x2, waiting for transfers between devices: none -> 66.1 us  [shards(): got = lax.ppermute(sent, ('occi', 'occj'), hops)]
    all_to_all x1 -> x0, blocking collectives: 29.8 us -> none  [shards(): lax.all_to_all(half.astype(jnp.bfloat16), ('occi', 'occj'), split_axis=1,...]
    all_to_all x1 -> x0, waiting for transfers between devices: 24.6 us -> none  [shards(): lax.all_to_all(outgoing.astype(jnp.bfloat16), ('occi', 'occj'), split_axi...]
    dot_general x1 -> x0, matrix products: 14.3 us -> none  [shards(): jnp.einsum('k,skab->sab', row_weights, lax.all_gather(amplitudes, 'occj',...]
    while x1 -> x0, local copies, waits for them, and re-layouts: 12.4 us -> none  [shards(): lax.map(lambda pair_in: pair_terms(pair_in[0], pair_in[1], thc_factor, th...]
    unnamed x0 -> x1, other arithmetic: none -> 11.1 us
    sub x0 -> x1, other arithmetic: none -> 10.3 us  [shards(): half = half - row_weights[k] * gathered[:, k].astype(jnp.float32)]
    unnamed x20 -> x18, local copies, waits for them, and re-layouts: 7.98 us -> 13.3 us
  transfers between devices with their start and end apart: 2 -> 3, of which waited for: 2 -> 3; matrix products, arithmetic and copies ran while one was open for 32% -> 31% of each run, Pallas kernels for 0% -> 0%
where the time goes in v1:
time: 201 us; the launch traced here: 200 us
  waiting for transfers between devices  91.5 us (46%)
  matrix products  46.5 us (23%)
  local copies, waits for them, and re-layouts  21.8 us (11%)
  other arithmetic  21.7 us (11%)
  between operations  14.2 us (7%)
  starting transfers between devices  4.8 us (2%)
    ppermute x2, waiting for transfers between devices, shards(): got = lax.ppermute(sent, ('occi', 'occj'), hops)  66.1 us
    all_gather x1, waiting for transfers between devices, shards(): gathered = lax.all_gather(amplitudes, 'occj', axis=1, tiled=True)  24.7 us
    dot_general x2, matrix products, pair_terms(): lax.dot_general(thc_factor, first, (((0,), (0,)), ((), ())), preferred_el...  21.4 us
    dot_general x2, matrix products, pair_terms(): lax.dot_general(second, thc_factor, (((1,), (1,)), ((), ())), preferred_e...  20.2 us
    unnamed x18, local copies, waits for them, and re-layouts  13.3 us
    unnamed x1, other arithmetic  11.1 us
    sub x1, other arithmetic, shards(): half = half - row_weights[k] * gathered[:, k].astype(jnp.float32)  10.3 us
    dot_general x2, matrix products, pair_terms(): virtual = jnp.dot(fock_vir, amp_pair, preferred_element_type=jnp.float32)  5 us
  transfers between devices with their start and end apart: 3, of which 3 were waited for; matrix products, arithmetic and copies ran while one was open for 31% of the time, Pallas kernels for 0%

profile of v1, /device:TPU:3, one launch (start us, length us, event | category | flops | bytes accessed | tf_op | source)
XLA Modules:
  0.0 200.5 jit_solution(9133931822053488868)
XLA Ops:
  7.2 0.0 copy-start
  7.2 0.0 all-gather.2.cloned.1.call-start
  7.2 0.7 all-gather.2.cloned.1.call-update
  7.9 0.8 copy.23
  8.7 12.5 %copy.22 = bf16[2048,2048]{0,1:T(8,128)(2,1)} copy(bf16[2048,2048]{1,0:T(8,128)(2,1)} %param.13) | data formatting | bytes 16777216 | tf_op args[3]
  21.2 0.0 copy-done.6
  21.2 0.1 convert_reduce_fusion
  21.3 0.0 copy-done.5
  21.4 0.7 fusion.27
  22.0 0.0 copy-done
  22.1 10.0 %fusion.1 = bf16[2048,2048]{0,1:T(8,128)(2,1)} fusion(bf16[2048,2048]{0,1:T(8,128)(2,1)} %copy.22, bf16[512,2048]{1,0:T(8,128)(2,1)S(1)} %copy-done, bf16[2,1,512,512]{3,2,1,0:T(8,128)(2,1)S(1)} %copy-done.2), kind=kOutput, calls=%fused_computation.3 | convolution fusion | flops 5382340608 | bytes 21495808 | tf_op jit(solution)/shard_map/dot_general | solution.py:18
  32.0 10.1 %convolution_add_fusion.2 = f32[512,512]{1,0:T(8,128)} fusion(bf16[512,2048]{1,0:T(8,128)(2,1)S(1)} %copy-done, bf16[2048,2048]{0,1:T(8,128)(2,1)} %fusion.1, bf16[2,1,512,512]{3,2,1,0:T(8,128)(2,1)} %param.11), kind=kOutput, calls=%fused_computation.24 | convolution fusion | flops 5370281984 | bytes 14155776 | tf_op jit(solution)/shard_map/dot_general | solution.py:23
  42.1 2.0 %fusion.11 = f32[1,512,512]{2,1,0:T(8,128)S(1)} fusion(f32[512,512]{1,0:T(8,128)} %convolution_add_fusion.2, bf16[512,512]{1,0:T(8,128)(2,1)} %param.14, bf16[2,1,512,512]{3,2,1,0:T(8,128)(2,1)} %param.10), kind=kOutput, calls=%fused_computation.21 | convolution fusion | flops 268697600 | bytes 3145728 | tf_op jit(solution)/shard_map/dot_general | solution.py:26
  44.1 11.4 %fusion = bf16[2048,2048]{0,1:T(8,128)(2,1)} fusion(bf16[2048,2048]{0,1:T(8,128)(2,1)} %copy.22, bf16[512,2048]{1,0:T(8,128)(2,1)S(1)} %copy-done, bf16[2,1,512,512]{3,2,1,0:T(8,128)(2,1)} %param.10), kind=kOutput, calls=%fused_computation.2 | convolution fusion | flops 5382340608 | bytes 21495808 | tf_op jit(solution)/shard_map/dot_general | solution.py:18
  55.5 10.1 %convolution_add_fusion.3 = f32[512,512]{1,0:T(8,128)} fusion(bf16[512,2048]{1,0:T(8,128)(2,1)S(1)} %copy-done, bf16[2048,2048]{0,1:T(8,128)(2,1)} %fusion, bf16[2,1,512,512]{3,2,1,0:T(8,128)(2,1)} %param.11), kind=kOutput, calls=%fused_computation.25 | convolution fusion | flops 5370281984 | bytes 14155776 | tf_op jit(solution)/shard_map/dot_general | solution.py:23
  65.6 3.0 %fusion.12 = f32[1,512,512]{2,1,0:T(8,128)} fusion(f32[512,512]{1,0:T(8,128)} %convolution_add_fusion.3, bf16[512,512]{1,0:T(8,128)(2,1)} %param.14, bf16[2,1,512,512]{3,2,1,0:T(8,128)(2,1)} %param.10), kind=kOutput, calls=%fused_computation.23 | convolution fusion | flops 268697600 | bytes 3145728 | tf_op jit(solution)/shard_map/dot_general | solution.py:26
  68.6 24.7 %all-gather.2.cloned.1.call-done = bf16[2,8,512,512]{3,2,0,1:T(8,128)(2,1)} async-done(((bf16[2,1,512,512]{3,2,0,1:T(8,128)(2,1)}), bf16[2,8,512,512]{3,2,0,1:T(8,128)(2,1)}) %all-gather.2.cloned.1.call-update) | async-done | bytes 8388624 | tf_op jit(solution)/shard_map/all_gather | solution.py:52
  93.3 10.3 %fusion.8 = f32[2,512,512]{2,1,0:T(8,128)} fusion(f32[1,512,512]{2,1,0:T(8,128)S(1)} %fusion.11, f32[1,512,512]{2,1,0:T(8,128)} %fusion.12, bf16[2,8,512,512]{3,2,0,1:T(8,128)(2,1)} %all-gather.2.cloned.1.call-done, f32[]{:T(128)} %bitcast.23, f32[]{:T(128)} %bitcast.21, f32[]{:T(128)} %bitcast.19, f32[]{:T(128)} %bitcast.17, f32[]{:T(128)} %bitcast.15, ...), kind=kLoop, calls=%fused_computation.15 | loop fusion | flops 13107200 | bytes 12582944 | tf_op jit(solution)/shard_map/sub | solution.py:59
  103.6 2.6 %copy.25 = bf16[2,512,512]{1,2,0:T(8,128)(2,1)} copy(f32[2,512,512]{2,1,0:T(8,128)} %fusion.8) | data formatting | bytes 3145728 | tf_op jit(solution)/shard_map/sub | solution.py:59
  106.2 2.2 %dynamic-slice_bitcast_fusion = (bf16[512,512]{1,0:T(8,128)(2,1)}, bf16[512,512]{1,0:T(8,128)(2,1)}) fusion(bf16[2,512,512]{1,2,0:T(8,128)(2,1)} %copy.25, s32[]{:T(128)S(6)} %select_n.42, s32[]{:T(128)S(6)} %select_n.38), kind=kLoop, calls=%fused_computation.34 | loop fusion | bytes 2097160 | tf_op jit(solution)/shard_map/jit(dynamic_index_in_dim)/squeeze | solution.py:68
  108.5 1.9 collective-permute-start
  110.4 2.9 %collective-permute-start.1 = (bf16[512,512]{1,0:T(8,128)(2,1)}, bf16[512,512]{1,0:T(8,128)(2,1)}, u32[]{:S(2)}, u32[]{:S(2)}) collective-permute-start(bf16[512,512]{1,0:T(8,128)(2,1)} %get-tuple-element.10), channel_id=1, source_target_pairs={{0,1},{1,0},{2,9},{3,8},{4,17},{5,16},{6,25},{7,24},{8,3},{9,2},{1... | collective-permute-start | bytes 1572872 | tf_op jit(solution)/shard_map/ppermute | solution.py:69
  113.2 0.6 dynamic_slice.20
  113.9 0.1 dynamic_slice.19
  114.0 0.0 copy-done.4
  114.0 0.1 broadcast_add_fusion
  114.1 55.6 %collective-permute-done = bf16[512,512]{1,0:T(8,128)(2,1)} collective-permute-done((bf16[512,512]{1,0:T(8,128)(2,1)}, bf16[512,512]{1,0:T(8,128)(2,1)}, u32[]{:S(2)}, u32[]{:S(2)}) %collective-permute-start) | collective-permute-done | bytes 524320 | tf_op jit(solution)/shard_map/ppermute | solution.py:69
  169.7 0.1 broadcast_in_dim.9
  169.8 1.1 bitcast_dynamic-update-slice_fusion.1
  170.9 10.5 %collective-permute-done.1 = bf16[512,512]{1,0:T(8,128)(2,1)} collective-permute-done((bf16[512,512]{1,0:T(8,128)(2,1)}, bf16[512,512]{1,0:T(8,128)(2,1)}, u32[]{:S(2)}, u32[]{:S(2)}) %collective-permute-start.1) | collective-permute-done | bytes 524320 | tf_op jit(solution)/shard_map/ppermute | solution.py:69
  181.4 1.1 bitcast_dynamic-update-slice_fusion
  182.5 11.1 %fusion.13 = (bf16[2,1,512,512]{3,2,1,0:T(8,128)(2,1)}, f32[2,1,512,512]{3,2,1,0:T(8,128)}) fusion(f32[]{:T(128)} %bitcast.35, f32[2]{0:T(128)S(1)} %dynamic_slice.19, f32[512,512]{1,0:T(8,128)S(1)} %broadcast_add_fusion, bf16[2,512,512]{2,1,0:T(8,128)(2,1)S(1)} %bitcast_dynamic-update-slice_fusion, bf16[2,1,512,512]{3,2,1,0:T(8,128)(2,1)S(1)} %copy-done.3, ...), kind=kLoop, calls=%fused_computation.26 | loop fusion | flops 17301504 | bytes 16777260
  (14 shorter events, 0.0 us)
Async XLA Ops:
  7.2 14.9 %copy-start = (bf16[512,2048]{1,0:T(8,128)(2,1)S(1)}, bf16[512,2048]{1,0:T(8,128)(2,1)}, u32[]{:S(2)}) copy-start(bf16[512,2048]{1,0:T(8,128)(2,1)} %param.12) | copy-start | bytes 6291460
  7.2 86.1 %all-gather.2.cloned.1.call-start = ((), (), s32[]{:S(2)}) async-start(), calls=%async_computation | async-start | bytes 9437184 | tf_op jit(solution)/shard_map/all_gather | solution.py:52
  8.7 12.5 %copy-start.6 = (s32[8]{0:T(128)S(1)}, s32[8]{0:T(128)}, u32[]{:S(2)}) copy-start(s32[8]{0:T(128)} %param.19) | copy-start | bytes 100
  8.7 12.6 %copy-start.5 = (f32[8,8]{1,0:T(8,128)S(1)}, f32[8,8]{1,0:T(8,128)}, u32[]{:S(2)}) copy-start(f32[8,8]{1,0:T(8,128)} %param.17) | copy-start | bytes 772
  8.7 13.3 %copy-start.2 = (bf16[2,1,512,512]{3,2,1,0:T(8,128)(2,1)S(1)}, bf16[2,1,512,512]{3,2,1,0:T(8,128)(2,1)}, u32[]{:S(2)}) copy-start(bf16[2,1,512,512]{3,2,1,0:T(8,128)(2,1)} %param.10) | copy-start | bytes 3145732
  103.6 9.6 %copy-start.7 = (f32[8]{0:T(128)S(1)}, f32[8]{0:T(128)}, u32[]{:S(2)}) copy-start(f32[8]{0:T(128)} %param.16) | copy-start | bytes 100
  103.6 10.4 %copy-start.4 = (f32[512]{0:T(512)S(1)}, f32[512]{0:T(512)}, u32[]{:S(2)}) copy-start(f32[512]{0:T(512)} %param.15) | copy-start | bytes 6148
  108.5 61.2 %collective-permute-start = (bf16[512,512]{1,0:T(8,128)(2,1)}, bf16[512,512]{1,0:T(8,128)(2,1)}, u32[]{:S(2)}, u32[]{:S(2)}) collective-permute-start(bf16[512,512]{1,0:T(8,128)(2,1)} %get-tuple-element.11), channel_id=1, source_target_pairs={{0,0},{1,1},{2,8},{3,9},{4,16},{5,17},{6,24},{7,25},{8,2},{9,3},{1... | collective-permute-start | bytes 1572872 | tf_op jit(solution)/shard_map/ppermute | solution.py:69
  110.4 71.0 %collective-permute-start.1 = (bf16[512,512]{1,0:T(8,128)(2,1)}, bf16[512,512]{1,0:T(8,128)(2,1)}, u32[]{:S(2)}, u32[]{:S(2)}) collective-permute-start(bf16[512,512]{1,0:T(8,128)(2,1)} %get-tuple-element.10), channel_id=1, source_target_pairs={{0,1},{1,0},{2,9},{3,8},{4,17},{5,16},{6,25},{7,24},{8,3},{9,2},{1... | collective-permute-start | bytes 1572872 | tf_op jit(solution)/shard_map/ppermute | solution.py:69
  114.0 68.5 %copy-start.1 = (f32[1,512,512]{2,1,0:T(8,128)S(1)}, f32[1,512,512]{2,1,0:T(8,128)}, u32[]{:S(2)}) copy-start(f32[1,512,512]{2,1,0:T(8,128)} %fusion.12) | copy-start | bytes 3145732
  114.0 68.5 %copy-start.3 = (bf16[2,1,512,512]{3,2,1,0:T(8,128)(2,1)S(1)}, bf16[2,1,512,512]{3,2,1,0:T(8,128)(2,1)}, u32[]{:S(2)}) copy-start(bf16[2,1,512,512]{3,2,1,0:T(8,128)(2,1)} %param.10) | copy-start | bytes 3145732
Sparse Core Ops, SparseCore 0:
  9.6 83.6 all-gather.1

commit v2 on v1

v2 whole, which is shorter than its diff:
```python
import functools

import jax
import jax.numpy as jnp
from jax import lax
from jax.experimental import pallas as pl
from jax.experimental.pallas import tpu as pltpu
from jax.sharding import PartitionSpec as P

MESH = pl.DeviceIdType.MESH
F32 = jnp.float32
BF16 = jnp.bfloat16


def coupling(fock_occ, couple_list, couple_count):
    n_occ = fock_occ.shape[0]
    slots = jnp.arange(couple_list.shape[1], dtype=jnp.int32)
    active = slots[None, :] < couple_count[:, None]
    target = jnp.arange(n_occ, dtype=jnp.int32)
    hits = (couple_list[:, :, None] == target[None, None, :]) & active[:, :, None]
    return fock_occ * jnp.sum(hits.astype(fock_occ.dtype), axis=1)


def tile_of(extent):
    return 512 if extent % 512 == 0 else extent


def kernel(
    n_first,
    n_second,
    amp_hbm,
    int_hbm,
    x_hbm,
    core_hbm,
    fock_hbm,
    weight_ref,
    occ_ref,
    row_ref,
    column_ref,
    residual_ref,
    updated_ref,
    pool,
    integral,
    x,
    xt,
    core,
    fock,
    first,
    scaled,
    half,
    part_out,
    part_in,
    turned,
    mirror,
    local_sem,
    gsend_sem,
    grecv_sem,
    relay_sem,
    psend_sem,
    precv_sem,
    msend_sem,
    mrecv_sem,
):
    rows, virt = half.shape[0], half.shape[1]
    rank = x.shape[1]
    near = n_second // 2
    tile = tile_of(rank)
    tiles = rank // tile
    chunk = 128
    a = lax.axis_index("occi")
    j = lax.axis_index("occj")
    mine = lax.rem(j, near)
    base = j - mine
    across = lax.rem(j + near, n_second)
    i_half = a // (n_first // 2)
    diagonal = i_half == j // near
    partner = mine + 1 - 2 * lax.rem(mine, 2)
    slot = lax.rem(j, rows)

    def signal(first_coord, second_coord):
        pl.semaphore_signal(
            pltpu.get_barrier_semaphore(),
            inc=1,
            device_id=(first_coord, second_coord),
            device_id_type=MESH,
        )

    for d in range(1, near):
        signal(a, base + lax.rem(mine + d, near))
    signal(a, across)
    for s in range(rows):
        pair_i = a * rows + s

        @pl.when(diagonal)
        def _():
            signal(across // rows, pair_i)

        @pl.when(jnp.logical_not(diagonal))
        def _():
            signal(j // rows, lax.rem(pair_i + near, n_second))

        @pl.when(pair_i != j)
        def _():
            signal(j // rows, pair_i)

    loads = [
        pltpu.make_async_copy(x_hbm, x, local_sem.at[0]),
        pltpu.make_async_copy(fock_hbm, fock, local_sem.at[1]),
        pltpu.make_async_copy(int_hbm, integral, local_sem.at[2]),
        pltpu.make_async_copy(core_hbm, core, local_sem.at[3]),
    ]
    own_loads = [
        pltpu.make_async_copy(amp_hbm.at[s], pool.at[s, mine], local_sem.at[4 + s])
        for s in range(rows)
    ]
    for load in own_loads + loads:
        load.start()
    self_pair = a == j // rows
    greeted = near + 2 * rows

    @pl.when(self_pair)
    def _():
        pl.semaphore_wait(pltpu.get_barrier_semaphore(), greeted - 1)

    @pl.when(jnp.logical_not(self_pair))
    def _():
        pl.semaphore_wait(pltpu.get_barrier_semaphore(), greeted)

    def gather_copy(s, d):
        peer = lax.rem(mine + d, near)
        return pltpu.make_async_remote_copy(
            src_ref=amp_hbm.at[s],
            dst_ref=pool.at[s, mine],
            send_sem=gsend_sem.at[s, d],
            recv_sem=grecv_sem.at[s, mine],
            device_id=(a, base + peer),
            device_id_type=MESH,
        )

    def partner_copy(s):
        return pltpu.make_async_remote_copy(
            src_ref=amp_hbm.at[s],
            dst_ref=pool.at[s, mine],
            send_sem=gsend_sem.at[s, 0],
            recv_sem=grecv_sem.at[s, mine],
            device_id=(a, base + partner),
            device_id_type=MESH,
        )

    def arrived(s, origin):
        pltpu.make_async_remote_copy(
            src_ref=amp_hbm.at[s],
            dst_ref=pool.at[s, origin],
            send_sem=gsend_sem.at[s, 0],
            recv_sem=grecv_sem.at[s, origin],
            device_id=(a, base + partner),
            device_id_type=MESH,
        ).wait_recv()

    def relay_copy(s, d):
        origin = lax.rem(mine + d, near)
        return pltpu.make_async_remote_copy(
            src_ref=pool.at[s, origin],
            dst_ref=pool.at[s, origin],
            send_sem=relay_sem.at[s, d],
            recv_sem=grecv_sem.at[s, origin],
            device_id=(a, base + partner),
            device_id_type=MESH,
        )

    far = range(2, near, 2)
    for s in range(rows):
        for d in far:
            gather_copy(s, d).start()
        partner_copy(s).start()

    loads[0].wait()
    for r in range(0, rank, tile):
        xt[pl.ds(r, tile), :] = x[:, pl.ds(r, tile)].T
    for load in own_loads + loads[1:3]:
        load.wait()
    for s in range(rows):
        half[s] = integral[s].astype(F32) + jnp.dot(
            fock[...], pool[s, mine], preferred_element_type=F32
        )
    loads[3].wait()

    def relay(s):
        for d in far:
            arrived(s, lax.rem(mine + d, near))
            relay_copy(s, d).start()

    def part_copy(s, to_mirror):
        if to_mirror:
            where, there = (across // rows, a * rows + s), lax.rem(across, rows)
        else:
            where, there = (a, across), s
        return pltpu.make_async_remote_copy(
            src_ref=part_out.at[s],
            dst_ref=part_in.at[there],
            send_sem=psend_sem.at[s],
            recv_sem=precv_sem.at[there],
            device_id=where,
            device_id_type=MESH,
        )

    def partial_sums(s):
        arrived(s, base * 0 + partner)
        for d in far:
            arrived(s, lax.rem(partner + near + d, near))

        @pl.loop(0, virt // chunk)
        def _(r):
            at = pl.ds(pl.multiple_of(r * chunk, chunk), chunk)
            own = jnp.zeros((chunk, virt), F32)
            other = jnp.zeros((chunk, virt), F32)
            for k in range(near):
                block = pool[s, k, at, :].astype(F32)
                own = own + weight_ref[0, k] * block
                other = other + weight_ref[1, k] * block
            half[s, at, :] = half[s, at, :] - own

            @pl.when(diagonal)
            def _():
                part_out[s, :, at] = other.T.astype(BF16)

            @pl.when(jnp.logical_not(diagonal))
            def _():
                part_out[s, at, :] = other.astype(BF16)

        @pl.when(diagonal)
        def _():
            part_copy(s, True).start()

        @pl.when(jnp.logical_not(diagonal))
        def _():
            part_copy(s, False).start()

    def mirror_copy(s):
        return pltpu.make_async_remote_copy(
            src_ref=turned.at[s],
            dst_ref=mirror.at[slot],
            send_sem=msend_sem.at[s],
            recv_sem=mrecv_sem.at[slot],
            device_id=(j // rows, a * rows + s),
            device_id_type=MESH,
        )

    def mirror_arrival(s):
        return pltpu.make_async_remote_copy(
            src_ref=turned.at[s],
            dst_ref=mirror.at[s],
            send_sem=msend_sem.at[s],
            recv_sem=mrecv_sem.at[s],
            device_id=(j // rows, a * rows + s),
            device_id_type=MESH,
        )

    def part_arrival(s):
        return pltpu.make_async_remote_copy(
            src_ref=part_out.at[s],
            dst_ref=part_in.at[s],
            send_sem=psend_sem.at[s],
            recv_sem=precv_sem.at[s],
            device_id=(a, across),
            device_id_type=MESH,
        )

    def send_half(s):
        part_arrival(s).wait_recv()

        @pl.loop(0, virt // chunk)
        def _(r):
            at = pl.ds(pl.multiple_of(r * chunk, chunk), chunk)
            rest = half[s, at, :] - part_in[s, at, :].astype(F32)
            half[s, at, :] = rest
            turned[s, :, at] = rest.T.astype(BF16)

        @pl.when(a * rows + s != j)
        def _():
            mirror_copy(s).start()

    steps = rows * tiles
    relay_at, sums_at, half_at = 1, min(3, steps - 1), min(tiles + 1, steps - 1)

    @pl.loop(0, steps)
    def _(step):
        s = lax.rem(j + step // tiles, rows)
        q = lax.rem(step, tiles)
        at_q = pl.ds(pl.multiple_of(q * tile, tile), tile)

        @pl.when(step == relay_at)
        def _():
            relay(0)

        @pl.when(step == relay_at + 1)
        def _():
            for s in range(1, rows):
                relay(s)

        @pl.when(step == sums_at)
        def _():
            @pl.loop(0, rows)
            def _(t):
                partial_sums(lax.rem(j + t, rows))

        @pl.when(jnp.logical_and(step == half_at, jnp.logical_not(diagonal)))
        def _():
            send_half(slot)

        first[...] = jnp.dot(
            pool[s, mine], x[:, at_q], preferred_element_type=F32
        ).astype(BF16)

        @pl.loop(0, tiles)
        def _(p):
            at_p = pl.ds(pl.multiple_of(p * tile, tile), tile)
            middle = jnp.dot(xt[at_p, :], first[...], preferred_element_type=F32)
            scaled[at_p, :] = (core[at_p, at_q].astype(F32) * middle).astype(BF16)

        second = jnp.dot(x[...], scaled[...], preferred_element_type=F32).astype(BF16)
        half[s] += lax.dot_general(
            second, x[:, at_q], (((1,), (1,)), ((), ())), preferred_element_type=F32
        )

    @pl.when(diagonal)
    def _():
        send_half(slot)

    @pl.loop(1, rows)
    def _(t):
        send_half(lax.rem(j + t, rows))

    @pl.loop(0, rows)
    def _(t):
        s = lax.rem(j + t, rows)
        local = a * rows + s == j

        def finish(source):
            @pl.loop(0, virt // chunk)
            def _(r):
                at = pl.ds(pl.multiple_of(r * chunk, chunk), chunk)
                total = half[s, at, :] + source[s, at, :].astype(F32)
                residual_ref[s, at, :] = total
                denominator = column_ref[at, :] + row_ref[...] - occ_ref[0, s] - occ_ref[1, s]
                updated_ref[s, at, :] = (
                    pool[s, mine, at, :].astype(F32) - total / denominator
                ).astype(BF16)

        @pl.when(local)
        def _():
            finish(turned)

        @pl.when(jnp.logical_not(local))
        def _():
            mirror_arrival(s).wait_recv()
            finish(mirror)
            mirror_copy(s).wait_send()

    for s in range(rows):
        for d in far:
            gather_copy(s, d).wait_send()
            relay_copy(s, d).wait_send()
        partner_copy(s).wait_send()
        part_arrival(s).wait_send()


def shards(
    amplitudes,
    exch_int,
    thc_factor,
    thc_core,
    fock_vir,
    eps_vir,
    eps_occ,
    fock_occ,
    couple_list,
    couple_count,
):
    rows = amplitudes.shape[0]
    virt = amplitudes.shape[2]
    rank = thc_factor.shape[1]
    n_first = lax.axis_size("occi")
    n_second = lax.axis_size("occj")
    near = n_second // 2
    a = lax.axis_index("occi")
    j = lax.axis_index("occj")
    weights = coupling(fock_occ, couple_list, couple_count)
    start = (j // near) * near
    own = lax.dynamic_slice(weights, (j, start), (1, near))
    other = lax.dynamic_slice(weights, ((j + near) % n_second, start), (1, near))
    weight = jnp.concatenate([own, other])
    occ = jnp.stack(
        [
            lax.dynamic_slice_in_dim(eps_occ, a * rows, rows, 0),
            jnp.broadcast_to(lax.dynamic_slice_in_dim(eps_occ, j, 1, 0), (rows,)),
        ]
    )
    anywhere = pl.BlockSpec(memory_space=pl.ANY)
    vmem = pl.BlockSpec(memory_space=pltpu.VMEM)
    smem = pl.BlockSpec(memory_space=pltpu.SMEM)
    tile = tile_of(rank)
    pair = (rows, virt, virt)
    dma = pltpu.SemaphoreType.DMA
    residual, updated = pl.pallas_call(
        functools.partial(kernel, n_first, n_second),
        out_shape=(jax.ShapeDtypeStruct(pair, F32), jax.ShapeDtypeStruct(pair, BF16)),
        in_specs=[anywhere] * 5 + [smem, smem, vmem, vmem],
        out_specs=(vmem, vmem),
        scratch_shapes=[
            pltpu.VMEM((rows, near, virt, virt), BF16),
            pltpu.VMEM(pair, BF16),
            pltpu.VMEM((virt, rank), BF16),
            pltpu.VMEM((rank, virt), BF16),
            pltpu.VMEM((rank, rank), BF16),
            pltpu.VMEM((virt, virt), BF16),
            pltpu.VMEM((virt, tile), BF16),
            pltpu.VMEM((rank, tile), BF16),
            pltpu.VMEM(pair, F32),
            pltpu.VMEM(pair, BF16),
            pltpu.VMEM(pair, BF16),
            pltpu.VMEM(pair, BF16),
            pltpu.VMEM(pair, BF16),
            dma((4 + rows,)),
            dma((rows, near)),
            dma((rows, near)),
            dma((rows, near)),
            dma((rows,)),
            dma((rows,)),
            dma((rows,)),
            dma((rows,)),
        ],
        compiler_params=pltpu.CompilerParams(
            collective_id=0, has_side_effects=True, vmem_limit_bytes=60 * 1024 * 1024
        ),
    )(
        amplitudes.reshape(pair),
        exch_int.reshape(pair),
        thc_factor,
        thc_core,
        fock_vir,
        weight,
        occ,
        eps_vir.reshape(1, virt),
        eps_vir.reshape(virt, 1),
    )
    return (residual.reshape(rows, 1, virt, virt), updated.reshape(rows, 1, virt, virt))


def solution(mesh):
    placed = (P("occi", "occj", None, None),) * 2 + (P(),) * 8
    return jax.shard_map(
        shards,
        mesh=mesh,
        in_specs=placed,
        out_specs=(P("occi", "occj", None, None), P("occi", "occj", None, None)),
        check_vma=False,
    )
```

time: 201 us -> 161 us (0.80)
  Pallas kernels: 0 us -> 148 us
  waiting for transfers between devices: 91.5 us -> 0 us
  matrix products: 46.5 us -> 0 us
  other arithmetic: 21.7 us -> 2.01 us
  between operations: 14.2 us -> 0.7 us
  local copies, waits for them, and re-layouts: 21.8 us -> 9.68 us
  starting transfers between devices: 4.8 us -> 0 us
    pallas_call x0 -> x1, Pallas kernels: none -> 148 us  [shards(): pl.pallas_call(functools.partial(kernel, n_first, n_second), out_shape=(j...]
    ppermute x2 -> x0, waiting for transfers between devices: 66.1 us -> none  [shards(): got = lax.ppermute(sent, ('occi', 'occj'), hops)]
    dot_general x6 -> x0, matrix products: 46.5 us -> none  [the longest x2 21.4 us: pair_terms(): lax.dot_general(thc_factor, first, (((0,), (0,)), ((), ())), preferred_el...]
    all_gather x1 -> x0, waiting for transfers between devices: 24.7 us -> none  [shards(): gathered = lax.all_gather(amplitudes, 'occj', axis=1, tiled=True)]
    unnamed x1 -> x0, other arithmetic: 11.1 us -> none
    sub x1 -> x0, other arithmetic: 10.3 us -> none  [shards(): half = half - row_weights[k] * gathered[:, k].astype(jnp.float32)]
    unnamed x18 -> x5, local copies, waits for them, and re-layouts: 13.3 us -> 4.91 us
    ppermute x2 -> x0, starting transfers between devices: 4.76 us -> none  [shards(): got = lax.ppermute(sent, ('occi', 'occj'), hops)]
  transfers between devices with their start and end apart: 3 -> 0, of which waited for: 3 -> 0; matrix products, arithmetic and copies ran while one was open for 31% -> 0% of each run, Pallas kernels for 0% -> 0%
where the time goes in v2:
time: 161 us
  Pallas kernels  148 us (92%)
  local copies, waits for them, and re-layouts  9.68 us (6%)
  other arithmetic  2.01 us (1%)
    pallas_call x1, Pallas kernels, shards(): pl.pallas_call(functools.partial(kernel, n_first, n_second), out_shape=(j...  148 us
    unnamed x5, local copies, waits for them, and re-layouts  4.91 us

profile of v2, /device:TPU:3, one launch (start us, length us, event | category | flops | bytes accessed | tf_op | source)
XLA Modules:
  0.0 160.7 jit_solution(14369048437783870735)
XLA Ops:
  0.7 1.2 dynamic_slice.17
  1.9 0.7 dynamic-slice_bitcast_fusion
  2.6 1.2 stack.7.occ_ref
  3.8 0.7 iota_compare_fusion.1
  4.5 0.8 copy.17
  5.3 0.1 convert_reduce_fusion
  5.3 0.7 mul.9
  6.0 0.1 fusion.1
  6.1 0.6 pad_maximum_fusion.weight_ref
  6.7 1.5 copy.18.column_ref
  8.2 148.3 %shard_map.113 = (f32[2,512,512]{2,1,0:T(8,128)}, bf16[2,512,512]{2,1,0:T(8,128)(2,1)}) custom-call(bf16[2,512,512]{2,1,0:T(8,128)(2,1)} %bitcast.14, bf16[2,512,512]{2,1,0:T(8,128)(2,1)} %bitcast.15, bf16[512,2048]{1,0:T(8,128)(2,1)} %x_hbm.1, bf16[2048,2048]{1,0:T(8,128)(2,1)} %core_hbm.1, bf16[512,512]{1,0:T(8,128)(2,1)} %fock_hbm.1, ...), custom_call_target="tpu_custom_call" | custom-call | tf_op jit(solution)/shard_map/pallas_call | solution.py:405
  156.5 0.0 copy-start
  156.5 3.2 %copy.23 = f32[2,1,512,512]{3,2,1,0:T(8,128)} copy(f32[2,1,512,512]{3,2,1,0:T(8,128)} %bitcast.13) | data formatting | bytes 4194304
  159.7 0.0 copy-done
  159.7 1.0 copy.24
Async XLA Ops:
  156.5 3.2 %copy-start = (bf16[2,512,512]{2,1,0:T(8,128)(2,1)S(1)}, bf16[2,512,512]{2,1,0:T(8,128)(2,1)}, u32[]{:S(2)}) copy-start(bf16[2,512,512]{2,1,0:T(8,128)(2,1)} %get-tuple-element.5) | copy-start | bytes 3145732

commit v3 on v2

--- a/solution.py
+++ b/solution.py
@@ -10,15 +10,6 @@
 MESH = pl.DeviceIdType.MESH
 F32 = jnp.float32
 BF16 = jnp.bfloat16
-
-
-def coupling(fock_occ, couple_list, couple_count):
-    n_occ = fock_occ.shape[0]
-    slots = jnp.arange(couple_list.shape[1], dtype=jnp.int32)
-    active = slots[None, :] < couple_count[:, None]
-    target = jnp.arange(n_occ, dtype=jnp.int32)
-    hits = (couple_list[:, :, None] == target[None, None, :]) & active[:, :, None]
-    return fock_occ * jnp.sum(hits.astype(fock_occ.dtype), axis=1)
 
 
 def tile_of(extent):
@@ -33,10 +24,11 @@
     x_hbm,
     core_hbm,
     fock_hbm,
-    weight_ref,
-    occ_ref,
     row_ref,
-    column_ref,
+    eps_ref,
+    fock_occ_ref,
+    list_ref,
+    count_ref,
     residual_ref,
     updated_ref,
     pool,
@@ -52,6 +44,8 @@
     part_in,
     turned,
     mirror,
+    passing,
+    part_pass,
     local_sem,
     gsend_sem,
     grecv_sem,
@@ -60,10 +54,17 @@
     precv_sem,
     msend_sem,
     mrecv_sem,
+    pass_sem,
+    low_send_sem,
+    low_recv_sem,
+    low_pass_sem,
+    low_done_sem,
 ):
     rows, virt = half.shape[0], half.shape[1]
     rank = x.shape[1]
     near = n_second // 2
+    upper = pl.ds(0, virt // 2)
+    lower = pl.ds(virt // 2, virt // 2)
     tile = tile_of(rank)
     tiles = rank // tile
     chunk = 128
@@ -76,6 +77,16 @@
     diagonal = i_half == j // near
     partner = mine + 1 - 2 * lax.rem(mine, 2)
     slot = lax.rem(j, rows)
+    flipped = lax.rem(a + n_first // 2, n_first)
+
+    def weight(orbital, k):
+        hits = jnp.float32(0.0)
+        for entry in range(list_ref.shape[1]):
+            active = jnp.logical_and(
+                list_ref[orbital, entry] == k, entry < count_ref[orbital]
+            )
+            hits = hits + jnp.where(active, jnp.float32(1.0), jnp.float32(0.0))
+        return hits * fock_occ_ref[orbital, k]
 
     def signal(first_coord, second_coord):
         pl.semaphore_signal(
@@ -88,6 +99,8 @@
     for d in range(1, near):
         signal(a, base + lax.rem(mine + d, near))
     signal(a, across)
+    signal(flipped, j)
+    signal(flipped, across)
     for s in range(rows):
         pair_i = a * rows + s
 
@@ -102,6 +115,14 @@
         @pl.when(pair_i != j)
         def _():
             signal(j // rows, pair_i)
+
+    @pl.when(diagonal)
+    def _():
+        signal(j // rows, flipped * rows + slot)
+
+    @pl.when(jnp.logical_not(diagonal))
+    def _():
+        signal(lax.rem(j // rows + n_first // 2, n_first), a * rows + slot)
 
     loads = [
         pltpu.make_async_copy(x_hbm, x, local_sem.at[0]),
@@ -116,7 +137,7 @@
     for load in own_loads + loads:
         load.start()
     self_pair = a == j // rows
-    greeted = near + 2 * rows
+    greeted = near + 2 * rows + 3
 
     @pl.when(self_pair)
     def _():
@@ -190,17 +211,44 @@
             arrived(s, lax.rem(mine + d, near))
             relay_copy(s, d).start()
 
-    def part_copy(s, to_mirror):
-        if to_mirror:
-            where, there = (across // rows, a * rows + s), lax.rem(across, rows)
-        else:
-            where, there = (a, across), s
+    def part_across(s):
+        return pltpu.make_async_remote_copy(
+            src_ref=part_out.at[s, upper],
+            dst_ref=part_in.at[s, upper],
+            send_sem=psend_sem.at[s],
+            recv_sem=precv_sem.at[s],
+            device_id=(a, across),
+            device_id_type=MESH,
+        )
+
+    def part_turned(s):
+        there = lax.rem(across, rows)
         return pltpu.make_async_remote_copy(
             src_ref=part_out.at[s],
             dst_ref=part_in.at[there],
             send_sem=psend_sem.at[s],
             recv_sem=precv_sem.at[there],
-            device_id=where,
+            device_id=(across // rows, a * rows + s),
+            device_id_type=MESH,
+        )
+
+    def low_to_flip(s):
+        return pltpu.make_async_remote_copy(
+            src_ref=part_out.at[s, lower],
+            dst_ref=part_pass.at[s],
+            send_sem=low_send_sem.at[s],
+            recv_sem=low_recv_sem.at[s],
+            device_id=(flipped, j),
+            device_id_type=MESH,
+        )
+
+    def low_on(s):
+        return pltpu.make_async_remote_copy(
+            src_ref=part_pass.at[s],
+            dst_ref=part_in.at[s, lower],
+            send_sem=low_pass_sem.at[s],
+            recv_sem=low_done_sem.at[s],
+            device_id=(flipped, across),
             device_id_type=MESH,
         )
 
@@ -208,6 +256,9 @@
         arrived(s, base * 0 + partner)
         for d in far:
             arrived(s, lax.rem(partner + near + d, near))
+
+        own_weights = [weight(j, base + k) for k in range(near)]
+        other_weights = [weight(across, base + k) for k in range(near)]
 
         @pl.loop(0, virt // chunk)
         def _(r):
@@ -216,8 +267,8 @@
             other = jnp.zeros((chunk, virt), F32)
             for k in range(near):
                 block = pool[s, k, at, :].astype(F32)
-                own = own + weight_ref[0, k] * block
-                other = other + weight_ref[1, k] * block
+                own = own + own_weights[k] * block
+                other = other + other_weights[k] * block
             half[s, at, :] = half[s, at, :] - own
 
             @pl.when(diagonal)
@@ -230,11 +281,12 @@
 
         @pl.when(diagonal)
         def _():
-            part_copy(s, True).start()
+            part_turned(s).start()
 
         @pl.when(jnp.logical_not(diagonal))
         def _():
-            part_copy(s, False).start()
+            low_to_flip(s).start()
+            part_across(s).start()
 
     def mirror_copy(s):
         return pltpu.make_async_remote_copy(
@@ -246,6 +298,26 @@
             device_id_type=MESH,
         )
 
+    def pass_on():
+        return pltpu.make_async_remote_copy(
+            src_ref=turned.at[slot],
+            dst_ref=passing,
+            send_sem=msend_sem.at[slot],
+            recv_sem=pass_sem.at[0],
+            device_id=(flipped, j),
+            device_id_type=MESH,
+        )
+
+    def pass_end():
+        return pltpu.make_async_remote_copy(
+            src_ref=passing,
+            dst_ref=mirror.at[slot],
+            send_sem=pass_sem.at[1],
+            recv_sem=mrecv_sem.at[slot],
+            device_id=(j // rows, flipped * rows + slot),
+            device_id_type=MESH,
+        )
+
     def mirror_arrival(s):
         return pltpu.make_async_remote_copy(
             src_ref=turned.at[s],
@@ -266,8 +338,15 @@
             device_id_type=MESH,
         )
 
-    def send_half(s):
-        part_arrival(s).wait_recv()
+    def send_half(s, passed):
+        @pl.when(diagonal)
+        def _():
+            part_across(s).wait_recv()
+            low_on(s).wait_recv()
+
+        @pl.when(jnp.logical_not(diagonal))
+        def _():
+            part_arrival(s).wait_recv()
 
         @pl.loop(0, virt // chunk)
         def _(r):
@@ -276,12 +355,17 @@
             half[s, at, :] = rest
             turned[s, :, at] = rest.T.astype(BF16)
 
-        @pl.when(a * rows + s != j)
-        def _():
-            mirror_copy(s).start()
+        if passed:
+            pass_on().start()
+        else:
+
+            @pl.when(a * rows + s != j)
+            def _():
+                mirror_copy(s).start()
 
     steps = rows * tiles
-    relay_at, sums_at, half_at = 1, min(3, steps - 1), min(tiles + 1, steps - 1)
+    half_at, late_at = tiles + 1, steps - 1
+    early = slot == 0
 
     @pl.loop(0, steps)
     def _(step):
@@ -289,24 +373,35 @@
         q = lax.rem(step, tiles)
         at_q = pl.ds(pl.multiple_of(q * tile, tile), tile)
 
-        @pl.when(step == relay_at)
-        def _():
-            relay(0)
-
-        @pl.when(step == relay_at + 1)
-        def _():
-            for s in range(1, rows):
-                relay(s)
-
-        @pl.when(step == sums_at)
-        def _():
-            @pl.loop(0, rows)
-            def _(t):
-                partial_sums(lax.rem(j + t, rows))
-
-        @pl.when(jnp.logical_and(step == half_at, jnp.logical_not(diagonal)))
-        def _():
-            send_half(slot)
+        for turn in range(rows):
+
+            @pl.when(step == 1 + 2 * turn)
+            def _():
+                relay(turn)
+
+            @pl.when(jnp.logical_and(step == 4 + 2 * turn, diagonal))
+            def _():
+                low_to_flip(turn).wait_recv()
+                low_on(turn).start()
+
+            @pl.when(step == 2 + 2 * turn)
+            def _():
+                partial_sums(turn)
+
+        sends = jnp.logical_or(
+            jnp.logical_and(step == half_at, early),
+            jnp.logical_and(step == late_at, jnp.logical_not(early)),
+        )
+
+        @pl.when(jnp.logical_and(sends, jnp.logical_not(diagonal)))
+        def _():
+            send_half(slot, True)
+
+        @pl.when(jnp.logical_and(step == late_at, jnp.logical_and(diagonal, early)))
+        def _():
+            pass_on().wait_recv()
+            pass_end().start()
+            send_half(slot, False)
 
         first[...] = jnp.dot(
             pool[s, mine], x[:, at_q], preferred_element_type=F32
@@ -323,13 +418,15 @@
             second, x[:, at_q], (((1,), (1,)), ((), ())), preferred_element_type=F32
         )
 
-    @pl.when(diagonal)
-    def _():
-        send_half(slot)
+    @pl.when(jnp.logical_and(diagonal, jnp.logical_not(early)))
+    def _():
+        pass_on().wait_recv()
+        pass_end().start()
+        send_half(slot, False)
 
     @pl.loop(1, rows)
     def _(t):
-        send_half(lax.rem(j + t, rows))
+        send_half(lax.rem(j + t, rows), False)
 
     @pl.loop(0, rows)
     def _(t):
@@ -342,7 +439,8 @@
                 at = pl.ds(pl.multiple_of(r * chunk, chunk), chunk)
                 total = half[s, at, :] + source[s, at, :].astype(F32)
                 residual_ref[s, at, :] = total
-                denominator = column_ref[at, :] + row_ref[...] - occ_ref[0, s] - occ_ref[1, s]
+                column = jnp.broadcast_to(row_ref[:, at], (chunk, chunk)).T[:, :1]
+                denominator = column + row_ref[...] - eps_ref[a * rows + s] - eps_ref[j]
                 updated_ref[s, at, :] = (
                     pool[s, mine, at, :].astype(F32) - total / denominator
                 ).astype(BF16)
@@ -362,7 +460,19 @@
             gather_copy(s, d).wait_send()
             relay_copy(s, d).wait_send()
         partner_copy(s).wait_send()
-        part_arrival(s).wait_send()
+
+    @pl.when(diagonal)
+    def _():
+        pass_end().wait_send()
+        for s in range(rows):
+            part_turned(s).wait_send()
+            low_on(s).wait_send()
+
+    @pl.when(jnp.logical_not(diagonal))
+    def _():
+        for s in range(rows):
+            part_across(s).wait_send()
+            low_to_flip(s).wait_send()
 
 
 def shards(
@@ -382,20 +492,6 @@
     rank = thc_factor.shape[1]
     n_first = lax.axis_size("occi")
     n_second = lax.axis_size("occj")
-    near = n_second // 2
-    a = lax.axis_index("occi")
-    j = lax.axis_index("occj")
-    weights = coupling(fock_occ, couple_list, couple_count)
-    start = (j // near) * near
-    own = lax.dynamic_slice(weights, (j, start), (1, near))
-    other = lax.dynamic_slice(weights, ((j + near) % n_second, start), (1, near))
-    weight = jnp.concatenate([own, other])
-    occ = jnp.stack(
-        [
-            lax.dynamic_slice_in_dim(eps_occ, a * rows, rows, 0),
-            jnp.broadcast_to(lax.dynamic_slice_in_dim(eps_occ, j, 1, 0), (rows,)),
-        ]
-    )
     anywhere = pl.BlockSpec(memory_space=pl.ANY)
     vmem = pl.BlockSpec(memory_space=pltpu.VMEM)
     smem = pl.BlockSpec(memory_space=pltpu.SMEM)
@@ -405,10 +501,10 @@
     residual, updated = pl.pallas_call(
         functools.partial(kernel, n_first, n_second),
         out_shape=(jax.ShapeDtypeStruct(pair, F32), jax.ShapeDtypeStruct(pair, BF16)),
-        in_specs=[anywhere] * 5 + [smem, smem, vmem, vmem],
+        in_specs=[anywhere] * 5 + [vmem] + [smem] * 4,
         out_specs=(vmem, vmem),
         scratch_shapes=[
-            pltpu.VMEM((rows, near, virt, virt), BF16),
+            pltpu.VMEM((rows, n_second // 2, virt, virt), BF16),
             pltpu.VMEM(pair, BF16),
             pltpu.VMEM((virt, rank), BF16),
             pltpu.VMEM((rank, virt), BF16),
@@ -421,10 +517,17 @@
             pltpu.VMEM(pair, BF16),
             pltpu.VMEM(pair, BF16),
             pltpu.VMEM(pair, BF16),
+            pltpu.VMEM((virt, virt), BF16),
+            pltpu.VMEM((rows, virt // 2, virt), BF16),
             dma((4 + rows,)),
-            dma((rows, near)),
-            dma((rows, near)),
-            dma((rows, near)),
+            dma((rows, n_second // 2)),
+            dma((rows, n_second // 2)),
+            dma((rows, n_second // 2)),
+            dma((rows,)),
+            dma((rows,)),
+            dma((rows,)),
+            dma((rows,)),
+            dma((2,)),
             dma((rows,)),
             dma((rows,)),
             dma((rows,)),
@@ -439,10 +542,11 @@
         thc_factor,
         thc_core,
         fock_vir,
-        weight,
-        occ,
         eps_vir.reshape(1, virt),
-        eps_vir.reshape(virt, 1),
+        eps_occ,
+        fock_occ,
+        couple_list,
+        couple_count,
     )
     return (residual.reshape(rows, 1, virt, virt), updated.reshape(rows, 1, virt, virt))
 

time: 161 us -> 118 us (0.73); the launches traced: 161 us -> 116 us
  Pallas kernels: 148 us -> 111 us
  local copies, waits for them, and re-layouts: 9.68 us -> 4.14 us
  other arithmetic: 2.01 us -> 0 us
    pallas_call x1, Pallas kernels: 148 us -> 111 us  [shards(): pl.pallas_call(functools.partial(kernel, n_first, n_second), out_shape=(j...]
    another operation x2 -> x0, local copies, waits for them, and re-layouts: 1.91 us -> none  [shards(): jnp.stack([lax.dynamic_slice_in_dim(eps_occ, a * rows, rows, 0), jnp.broa...]
    unnamed x5 -> x4, local copies, waits for them, and re-layouts: 4.91 us -> 4.14 us
where the time goes in v3:
time: 118 us; the launch traced here: 116 us
  Pallas kernels  111 us (94%)
  local copies, waits for them, and re-layouts  4.14 us (4%)
    pallas_call x1, Pallas kernels, shards(): pl.pallas_call(functools.partial(kernel, n_first, n_second), out_shape=(j...  111 us
    unnamed x4, local copies, waits for them, and re-layouts  4.14 us

profile of v3, /device:TPU:3, one launch (start us, length us, event | category | flops | bytes accessed | tf_op | source)
XLA Modules:
  0.0 115.6 jit_solution(13772893763226126456)
XLA Ops:
  0.6 110.8 %shard_map.113 = (f32[2,512,512]{2,1,0:T(8,128)}, bf16[2,512,512]{2,1,0:T(8,128)(2,1)}) custom-call(bf16[2,512,512]{2,1,0:T(8,128)(2,1)} %bitcast.10, bf16[2,512,512]{2,1,0:T(8,128)(2,1)} %bitcast.11, bf16[512,2048]{1,0:T(8,128)(2,1)} %x_hbm.1, bf16[2048,2048]{1,0:T(8,128)(2,1)} %core_hbm.1, bf16[512,512]{1,0:T(8,128)(2,1)} %fock_hbm.1, f32[1,512]{1,0:T(1,128)} %bitcast.13, ...), custom_call_target="tpu_custom_call" | custom-call | tf_op jit(solution)/shard_map/pallas_call | solution.py:501
  111.4 0.0 copy-start
  111.4 3.2 %copy.16 = f32[2,1,512,512]{3,2,1,0:T(8,128)} copy(f32[2,1,512,512]{3,2,1,0:T(8,128)} %bitcast.9) | data formatting | bytes 4194304
  114.6 0.0 copy-done
  114.6 1.0 copy.17
Async XLA Ops:
  111.4 3.2 %copy-start = (bf16[2,512,512]{2,1,0:T(8,128)(2,1)S(1)}, bf16[2,512,512]{2,1,0:T(8,128)(2,1)}, u32[]{:S(2)}) copy-start(bf16[2,512,512]{2,1,0:T(8,128)(2,1)} %get-tuple-element.5) | copy-start | bytes 3145732

commit v4 on v3

--- a/solution.py
+++ b/solution.py
@@ -399,9 +399,9 @@
 
         @pl.when(jnp.logical_and(step == late_at, jnp.logical_and(diagonal, early)))
         def _():
+            send_half(slot, False)
             pass_on().wait_recv()
             pass_end().start()
-            send_half(slot, False)
 
         first[...] = jnp.dot(
             pool[s, mine], x[:, at_q], preferred_element_type=F32
@@ -420,13 +420,16 @@
 
     @pl.when(jnp.logical_and(diagonal, jnp.logical_not(early)))
     def _():
-        pass_on().wait_recv()
-        pass_end().start()
         send_half(slot, False)
 
     @pl.loop(1, rows)
     def _(t):
         send_half(lax.rem(j + t, rows), False)
+
+    @pl.when(jnp.logical_and(diagonal, jnp.logical_not(early)))
+    def _():
+        pass_on().wait_recv()
+        pass_end().start()
 
     @pl.loop(0, rows)
     def _(t):

time: 118 us -> 116 us (0.983); the launches traced: 116 us -> 116 us
  no operation moved by 1% of the time
where the time goes in v4:
time: 116 us
  Pallas kernels  111 us (96%)
  local copies, waits for them, and re-layouts  4.14 us (4%)
    pallas_call x1, Pallas kernels, shards(): pl.pallas_call(functools.partial(kernel, n_first, n_second), out_shape=(j...  111 us
    unnamed x4, local copies, waits for them, and re-layouts  4.14 us

profile of v4, /device:TPU:3, one launch (start us, length us, event | category | flops | bytes accessed | tf_op | source)
XLA Modules:
  0.0 115.6 jit_solution(8608191603067360404)
XLA Ops:
  0.6 110.8 %shard_map.113 = (f32[2,512,512]{2,1,0:T(8,128)}, bf16[2,512,512]{2,1,0:T(8,128)(2,1)}) custom-call(bf16[2,512,512]{2,1,0:T(8,128)(2,1)} %bitcast.10, bf16[2,512,512]{2,1,0:T(8,128)(2,1)} %bitcast.11, bf16[512,2048]{1,0:T(8,128)(2,1)} %x_hbm.1, bf16[2048,2048]{1,0:T(8,128)(2,1)} %core_hbm.1, bf16[512,512]{1,0:T(8,128)(2,1)} %fock_hbm.1, f32[1,512]{1,0:T(1,128)} %bitcast.13, ...), custom_call_target="tpu_custom_call" | custom-call | tf_op jit(solution)/shard_map/pallas_call | solution.py:504
  111.4 0.0 copy-start
  111.4 3.2 %copy.16 = f32[2,1,512,512]{3,2,1,0:T(8,128)} copy(f32[2,1,512,512]{3,2,1,0:T(8,128)} %bitcast.9) | data formatting | bytes 4194304
  114.6 0.0 copy-done
  114.6 1.0 copy.17
Async XLA Ops:
  111.4 3.2 %copy-start = (bf16[2,512,512]{2,1,0:T(8,128)(2,1)S(1)}, bf16[2,512,512]{2,1,0:T(8,128)(2,1)}, u32[]{:S(2)}) copy-start(bf16[2,512,512]{2,1,0:T(8,128)(2,1)} %get-tuple-element.5) | copy-start | bytes 3145732
